TPU v7x, 32 devices: a whole 2x2x4 slice. The times are simulated.
32 devices in a mesh: member: 8 (over z, x), cell: 4 (over y, core).
Axes of the slice: x: 2, y: 2, z: 4, core: 2. Of those that a mesh axis runs over, the one named last changes fastest.
Arguments:
- latent: bfloat16 [8, 6144, 1024], P('member', 'cell'), may hold values from -6 to 6
- w_in: bfloat16 [1024, 1024], replicated, may hold values from -0.1875 to 0.1875
- w_out: bfloat16 [1024, 96], replicated, may hold values from -0.1875 to 0.1875
- target: bfloat16 [96, 6144], P(None, 'cell'), may hold values from -6 to 6
- cell_mask: int32 [6144], P('cell'), may hold values 0 or 1
Outputs:
- grad_w_in: float32 [1024, 1024], P(('member', 'cell'))
- grad_w_out: float32 [1024, 96], P(('member', 'cell'))
All inputs are finite; a program needn't handle non-finite values. No bound on the sum of `cell_mask` on one device may be relied on, other than what follows from the above.
Results may differ from a plain program's by a relative error of at most 0.0055.
Values may be sent and summed in bfloat16 or wider, within the bound.
A program may use at most 64 MiB of HBM per device.

v0:
```python
import jax
import jax.numpy as jnp
from jax import lax
from jax.sharding import PartitionSpec as P


def kernel_fn(diff):
    return diff / jnp.sqrt(1.0 + diff * diff)


def silu_slope(pre):
    gate = jax.nn.sigmoid(pre)
    return gate * (1.0 + pre * (1.0 - gate))


def per_device(latent, w_in, w_out, target, cell_mask):
    members = lax.axis_size("member")
    cell_count = lax.axis_size("cell")
    own_latent = latent[0]
    cells_here = own_latent.shape[0]
    scale = 1.0 / jnp.sqrt(jnp.float32(cells_here * cell_count))
    pre = jnp.dot(own_latent, w_in, preferred_element_type=jnp.float32)
    hidden = jax.nn.silu(pre).astype(jnp.bfloat16)
    fields = lax.dot_general(
        w_out, hidden, (((0,), (1,)), ((), ())), preferred_element_type=jnp.float32
    ).astype(jnp.bfloat16)
    wide = fields.astype(jnp.float32)
    pair = jnp.sum(
        kernel_fn(
            wide[None]
            - lax.all_gather(fields[None], "member", axis=0, tiled=True).astype(jnp.float32)
        ),
        axis=0,
    )
    weight = cell_mask.astype(jnp.float32) * scale / members
    own_term = kernel_fn(wide - target.astype(jnp.float32))
    grad_fields = (weight[None] * (own_term - pair / members)).astype(jnp.bfloat16)
    back = lax.dot_general(
        grad_fields, w_out, (((0,), (1,)), ((), ())), preferred_element_type=jnp.float32
    )
    grad_pre = (back * silu_slope(pre)).astype(jnp.bfloat16)
    width = w_in.shape[1]
    grad_in = lax.dot_general(
        own_latent, grad_pre, (((0,), (0,)), ((), ())), preferred_element_type=jnp.float32
    )
    grad_out = lax.dot_general(
        hidden, grad_fields, (((0,), (1,)), ((), ())), preferred_element_type=jnp.float32
    )
    owned = lax.psum_scatter(
        jnp.concatenate([grad_in, grad_out], axis=1),
        ("member", "cell"),
        scatter_dimension=0,
        tiled=True,
    )
    return (owned[:, :width], owned[:, width:])


def solution(mesh):
    in_specs = (P("member", "cell", None), P(), P(), P(None, "cell"), P("cell"))
    out_specs = (P(("member", "cell"), None), P(("member", "cell"), None))
    return jax.shard_map(
        per_device, mesh=mesh, in_specs=in_specs, out_specs=out_specs, check_vma=False
    )
```

profile of v0, /device:TPU:0, one launch (start us, length us, event | category | flops | bytes accessed | tf_op | source)
XLA Modules:
  0.0 217.5 jit_solution(14600535981441059085)
XLA Ops:
  7.2 0.0 copy-start
  7.2 0.0 all-gather.3.cloned.1.call-start
  7.2 1.8 copy-done
  9.1 0.0 copy-start.5
  9.1 7.5 %multiply_convert_fusion.1 = (bf16[1536,1024]{1,0:T(8,128)(2,1)S(1)}, f32[1536,1024]{1,0:T(8,128)}) fusion(bf16[1024,1024]{1,0:T(8,128)(2,1)} %param.6, bf16[1,1536,1024]{2,1,0:T(8,128)(2,1)S(1)} %copy-done), kind=kOutput, calls=%fused_computation.1 | convolution fusion | flops 3229089792 | bytes 14680064 | tf_op jit(solution)/shard_map/dot_general | solution.py:22
  16.6 0.0 copy-start.1
  16.6 0.0 copy-start.6
  16.6 1.7 copy-done.1
  18.3 0.0 copy-done.5
  18.3 0.0 copy-start.4
  18.3 2.0 fusion.14
  20.3 0.0 all-gather.3.cloned.1.call-update
  20.4 0.0 reduce-scatter.4.cloned.1.call-start
  20.4 0.0 copy-done.6
  20.4 54.6 %all-gather.3.cloned.1.call-done = bf16[768,1536]{1,0:T(8,128)(2,1)} async-done(((bf16[96,1536]{1,0:T(8,128)(2,1)}), bf16[768,1536]{1,0:T(8,128)(2,1)}) %all-gather.3.cloned.1.call-update) | async-done | bytes 2359312 | tf_op jit(solution)/shard_map/all_gather | solution.py:31
  75.0 0.0 copy-start.2
  75.1 3.1 %fusion.4 = f32[96,1536]{1,0:T(8,128)S(1)} fusion(bf16[8,96,1536]{2,1,0:T(8,128)(2,1)} %bitcast.23, f32[96,1536]{1,0:T(8,128)} %get-tuple-element.8), kind=kLoop, calls=%fused_computation.8 | loop fusion | flops 6930432 | bytes 3538944 | tf_op jit(solution)/shard_map/reduce_sum | solution.py:28
  78.1 0.0 copy-done.4
  78.1 1.2 multiply_convert_fusion.2
  79.3 0.0 copy-done.2
  79.3 0.0 copy-start.3
  79.3 0.6 fusion.15
  80.0 0.1 copy-done.3
  80.0 10.6 %fusion.10 = f32[1024,1024]{0,1:T(8,128)} fusion(bf16[1,1536,1024]{2,1,0:T(8,128)(2,1)S(1)} %copy-done, f32[1536,1024]{1,0:T(8,128)} %get-tuple-element.7, bf16[96,1536]{1,0:T(8,128)(2,1)} %copy-done.3, bf16[1024,96]{0,1:T(8,128)(2,1)} %param.7), kind=kOutput, calls=%fused_computation.16 | convolution fusion | flops 3537371136 | bytes 14123008 | tf_op jit(solution)/shard_map/dot_general | solution.py:43
  90.7 5.0 %pad_maximum_fusion = f32[1024,1120]{0,1:T(8,128)} fusion(f32[1024,96]{0,1:T(8,128)S(1)} %fusion.15, f32[1024,1024]{0,1:T(8,128)} %fusion.10), kind=kLoop, calls=%fused_computation.9 | loop fusion | flops 1146880 | bytes 9175040 | tf_op jit(solution)/shard_map/concatenate | solution.py:50
  95.7 5.9 %copy.11 = f32[1024,1120]{1,0:T(8,128)} copy(f32[1024,1120]{0,1:T(8,128)} %pad_maximum_fusion) | data formatting | bytes 9175040
  101.6 0.0 reduce-scatter.4.cloned.1.call-update
  101.6 106.2 %reduce-scatter.4.cloned.1.call-done = f32[32,1120]{1,0:T(8,128)} async-done(((f32[1024,1120]{1,0:T(8,128)}), f32[32,1120]{1,0:T(8,128)}) %reduce-scatter.4.cloned.1.call-update) | async-done | bytes 143376
  207.8 1.6 slice.8
  209.3 1.3 slice.9
  (1 shorter events, 0.0 us)
Async XLA Ops:
  7.2 1.9 copy-start
  7.2 67.9 %all-gather.3.cloned.1.call-start = ((), (), s32[]{:S(2)}) async-start(), calls=%async_computation.1 | async-start | bytes 2654208 | tf_op jit(solution)/shard_map/all_gather | solution.py:31
  9.1 9.2 %copy-start.5 = (bf16[1024,96]{0,1:T(8,128)(2,1)S(1)}, bf16[1024,96]{0,1:T(8,128)(2,1)}, u32[]{:S(2)}) copy-start(bf16[1024,96]{0,1:T(8,128)(2,1)} %param.7) | copy-start | bytes 589828
  16.6 1.7 copy-start.1
  16.6 3.8 %copy-start.6 = (s32[1536]{0:T(1024)S(1)}, s32[1536]{0:T(1024)}, u32[]{:S(2)}) copy-start(s32[1536]{0:T(1024)} %param.9) | copy-start | bytes 18436
  18.3 59.8 %copy-start.4 = (bf16[96,1536]{1,0:T(8,128)(2,1)S(1)}, bf16[96,1536]{1,0:T(8,128)(2,1)}, u32[]{:S(2)}) copy-start(bf16[96,1536]{1,0:T(8,128)(2,1)} %param.8) | copy-start | bytes 884740
  20.4 187.4 %reduce-scatter.4.cloned.1.call-start = ((), (), s32[]{:S(2)}) async-start(), calls=%async_computation.2 | async-start | bytes 4866048
  75.0 4.3 %copy-start.2 = (bf16[1536,1024]{1,0:T(8,128)(2,1)S(1)}, bf16[1536,1024]{1,0:T(8,128)(2,1)}, u32[]{:S(2)}) copy-start(bf16[1536,1024]{1,0:T(8,128)(2,1)} %copy-done.1) | copy-start | bytes 9437188
  79.3 0.7 copy-start.3
Sparse Core Ops, SparseCore 0:
  20.5 54.5 all-gather.2
  101.7 105.9 reduce-scatter.3
where the time goes:
time: 218 us
  waiting for transfers between devices  161 us (74%)
  matrix products  20.8 us (10%)
  between operations  14.1 us (6%)
  local copies, waits for them, and re-layouts  12.5 us (6%)
  other arithmetic  9.23 us (4%)
    unnamed x3, waiting for transfers between devices  106 us
    all_gather x1, waiting for transfers between devices, per_device(): lax.all_gather(fields[None], 'member', axis=0, tiled=True)  54.6 us
    dot_general x1, matrix products, per_device(): lax.dot_general(own_latent, grad_pre, (((0,), (0,)), ((), ())), preferred...  10.6 us
    unnamed x15, local copies, waits for them, and re-layouts  9.56 us
    dot_general x1, matrix products, per_device(): pre = jnp.dot(own_latent, w_in, preferred_element_type=jnp.float32)  7.54 us
    concatenate x1, other arithmetic, per_device(): jnp.concatenate([grad_in, grad_out], axis=1)  4.99 us
  transfers between devices with their start and end apart: 2, of which 2 were waited for; matrix products, arithmetic and copies ran while one was open for 0% of the time, Pallas kernels for 0%

commit v1 on v0

v1 whole, which is shorter than its diff:
```python
import functools

import jax
import jax.numpy as jnp
from jax import lax
from jax.experimental import pallas as pl
from jax.experimental.pallas import tpu as pltpu
from jax.sharding import PartitionSpec as P

MESH = pl.DeviceIdType.MESH
BF = jnp.bfloat16
F32 = jnp.float32


def sigmoid(v):
    return 0.5 * jnp.tanh(0.5 * v) + 0.5


def smooth(d):
    return d * lax.rsqrt(1.0 + d * d)


def mm(a, b):
    return jnp.dot(a, b, preferred_element_type=F32)


def body(
    M, CN,
    lat, w_in, w_out, target, mask, out_in, out_out,
    pre, hid, gp, lat_t, hid_t, tgt_t, wgt_t,
    fsend, frecv, gsend, gf,
    acc_f, acc_b, r1, k2, s2, r2, s3, r3, k3,
    sem_fs, sem_fr, sem_gs, sem_gr, sem1s, sem1r, sem2s, sem2r, sem3s, sem3r,
):
    me = lax.axis_index("member")
    cell = lax.axis_index("cell")
    core = lax.rem(cell, 2)
    grp = cell // 2
    G = CN // 2
    N, D = lat.shape
    H = w_in.shape[1]
    FD = w_out.shape[1]
    C = N // M
    PB = M // 2
    r = D // (M * CN)
    scale = 1.0 / (float(N * CN) ** 0.5) / M

    barrier = pltpu.get_barrier_semaphore()
    for d in range(1, M):
        pl.semaphore_signal(barrier, inc=1, device_id=(lax.rem(me + d, M), cell), device_id_type=MESH)
    pl.semaphore_signal(barrier, inc=1, device_id=(me, grp * 2 + 1 - core), device_id_type=MESH)
    for d in range(1, G):
        pl.semaphore_signal(
            barrier, inc=1, device_id=(me, lax.rem(grp + d, G) * 2 + core), device_id_type=MESH
        )
    pl.semaphore_wait(barrier, M - 1 + 1 + G - 1)

    def peer(d):
        return lax.rem(me + d, M)

    def f_copy(d):
        return pltpu.make_async_remote_copy(
            fsend.at[peer(d)], frecv.at[d - 1], sem_fs.at[d - 1], sem_fr.at[d - 1],
            device_id=(peer(d), cell), device_id_type=MESH,
        )

    def g_copy(d):
        return pltpu.make_async_remote_copy(
            gsend.at[d - 1], gf.at[me], sem_gs.at[d - 1], sem_gr.at[d - 1],
            device_id=(lax.rem(me - d + M, M), cell), device_id_type=MESH,
        )

    def c1(i):
        return pltpu.make_async_remote_copy(
            acc_b.at[i, 1 - core], r1.at[i], sem1s.at[i], sem1r.at[i],
            device_id=(me, grp * 2 + 1 - core), device_id_type=MESH,
        )

    def c2(i, d):
        g = lax.rem(grp + d, G)
        return pltpu.make_async_remote_copy(
            s2.at[i, g], r2.at[i, d - 1], sem2s.at[i, d - 1], sem2r.at[i, d - 1],
            device_id=(me, g * 2 + core), device_id_type=MESH,
        )

    def c3(t):
        d = lax.rem(t - me + M, M)
        return pltpu.make_async_remote_copy(
            s3.at[t], r3.at[d - 1], sem3s.at[d - 1], sem3r.at[d - 1],
            device_id=(t, cell), device_id_type=MESH,
        )

    def block_of(i):
        return lax.rem(me // 2 + 1 + i, PB)

    def forward(i, carry):
        p = block_of(i)
        rows = pl.ds(pl.multiple_of(p * (2 * C), 2 * C), 2 * C)
        v = mm(lat[rows, :], w_in[...])
        pre[rows, :] = v
        h = (v * sigmoid(v)).astype(BF)
        hid[rows, :] = h
        f = mm(h, w_out[...]).astype(BF)
        fsend[2 * p] = f[:C]
        fsend[2 * p + 1] = f[C:]
        for s in range(2):
            t = 2 * p + s

            @pl.when(t != me)
            def _():
                f_copy(lax.rem(t - me + M, M)).start()

        return carry

    lax.fori_loop(0, PB, forward, 0)

    wrow = mask[...].astype(F32) * scale
    for b in range(N // 128):
        cols = slice(128 * b, 128 * b + 128)
        tgt_t[cols, :] = target[:, cols].astype(F32).T
        wgt_t[cols, :] = jnp.broadcast_to(wrow[:, cols], (8, 128)).T

    for b in range(N // 128):
        cols = slice(128 * b, 128 * b + 128)
        lat_t[:, cols] = lat[cols, :].T

    for d in range(1, M):
        f_copy(d).wait_recv()

    RB = 16

    def pairs(b, carry):
        rows = pl.ds(pl.multiple_of(b * RB, RB), RB)
        own = pl.ds(pl.multiple_of(me * C + b * RB, RB), RB)
        vals = [frecv[j, rows, :].astype(F32) for j in range(M - 1)]
        vals.append(fsend[me, rows, :].astype(F32))
        t = tgt_t[own, :]
        w = wgt_t[own, 0:1]
        total = [None] * M
        for a in range(M):
            for c in range(a + 1, M):
                k = smooth(vals[a] - vals[c])
                total[a] = k if total[a] is None else total[a] + k
                total[c] = -k if total[c] is None else total[c] - k
        for a in range(M):
            g = (w * (smooth(vals[a] - t) - total[a] * (1.0 / M))).astype(BF)
            if a < M - 1:
                gsend[a, rows, :] = g
            else:
                gf[me, rows, :] = g
        return carry

    lax.fori_loop(0, C // RB, pairs, 0)

    for d in range(1, M):
        g_copy(d).start()

    for b in range(N // 128):
        cols = slice(128 * b, 128 * b + 128)
        hid_t[:, cols] = hid[cols, :].T

    def back(j):
        rows = pl.ds(pl.multiple_of(j * C, C), C)
        q = lax.dot_general(gf[j], w_out[...], (((1,), (1,)), ((), ())), preferred_element_type=F32)
        v = pre[rows, :]
        s = sigmoid(v)
        gp[rows, :] = (q * (s * (1.0 + v * (1.0 - s)))).astype(BF)

    back(me)

    def backs(d, carry):
        pltpu.make_async_remote_copy(
            gsend.at[d - 1], gf.at[lax.rem(me + d, M)], sem_gs.at[d - 1], sem_gr.at[d - 1],
            device_id=(peer(d), cell), device_id_type=MESH,
        ).wait_recv()
        back(lax.rem(me + d, M))
        return carry

    lax.fori_loop(1, M, backs, 0)

    def step(i, carry):
        @pl.when(i < PB)
        def _():
            p = block_of(i)
            rows = pl.ds(pl.multiple_of(p * (2 * r * CN), 2 * r * CN), 2 * r * CN)
            a = mm(lat_t[rows, :], gp[...])
            b = mm(hid_t[rows, :], gf[...].reshape(N, FD))
            for s in range(2):
                for c in range(CN):
                    at = (s * CN + c) * r
                    x, y = a[at : at + r], b[at : at + r]
                    acc_f[i, c % 2, s, c // 2, :, :H] = x
                    acc_f[i, c % 2, s, c // 2, :, H : H + FD] = y
                    acc_b[i, c % 2, s, c // 2, :, :H] = x.astype(BF)
                    acc_b[i, c % 2, s, c // 2, :, H : H + FD] = y.astype(BF)
            c1(i).start()

        @pl.when((i >= 1) & (i <= PB))
        def _():
            j = i - 1
            c1(j).wait_recv()
            for g in range(G):
                for s in range(2):
                    v = acc_f[j, core, s, g] + r1[j, s, g].astype(F32)
                    k2[j, g, s] = v
                    s2[j, g, s] = v.astype(BF)
            for d in range(1, G):
                c2(j, d).start()

        @pl.when(i >= 2)
        def _():
            j = i - 2
            p = block_of(j)
            for d in range(1, G):
                c2(j, d).wait_recv()
            for s in range(2):
                v = k2[j, grp, s]
                for d in range(1, G):
                    v = v + r2[j, d - 1, s].astype(F32)
                t = 2 * p + s
                s3[t] = v.astype(BF)

                @pl.when(t == me)
                def _():
                    k3[...] = v

                @pl.when(t != me)
                def _():
                    c3(t).start()

        return carry

    lax.fori_loop(0, PB + 2, step, 0)

    total = k3[...]
    for d in range(1, M):
        pltpu.make_async_remote_copy(
            s3.at[0], r3.at[d - 1], sem3s.at[d - 1], sem3r.at[d - 1],
            device_id=(peer(d), cell), device_id_type=MESH,
        ).wait_recv()
        total = total + r3[d - 1].astype(F32)
    out_in[...] = total[:, :H]
    out_out[...] = total[:, H : H + FD]

    for d in range(1, M):
        f_copy(d).wait_send()
        g_copy(d).wait_send()
        c3(peer(d)).wait_send()
    for i in range(PB):
        c1(i).wait_send()
        for d in range(1, G):
            c2(i, d).wait_send()


def per_device(latent, w_in, w_out, target, cell_mask):
    M = lax.axis_size("member")
    CN = lax.axis_size("cell")
    N, D = latent.shape[1:]
    H = w_in.shape[1]
    FD = w_out.shape[1]
    C, PB, G = N // M, M // 2, CN // 2
    r = D // (M * CN)
    W = H + (FD + 127) // 128 * 128
    V = pltpu.VMEM
    DMA = pltpu.SemaphoreType.DMA
    GS = max(G - 1, 1)
    vm = pl.BlockSpec(memory_space=pltpu.VMEM)
    return pl.pallas_call(
        functools.partial(body, M, CN),
        out_shape=(
            jax.ShapeDtypeStruct((r, H), F32),
            jax.ShapeDtypeStruct((r, FD), F32),
        ),
        in_specs=[vm] * 5,
        out_specs=(vm, vm),
        scratch_shapes=[
            V((N, H), F32), V((N, H), BF), V((N, H), BF), V((D, N), BF), V((H, N), BF),
            V((N, FD), F32), V((N, 8), F32),
            V((M, C, FD), BF), V((M - 1, C, FD), BF), V((M - 1, C, FD), BF), V((M, C, FD), BF),
            V((PB, 2, 2, G, r, W), F32), V((PB, 2, 2, G, r, W), BF), V((PB, 2, G, r, W), BF),
            V((PB, G, 2, r, W), F32), V((PB, G, 2, r, W), BF), V((PB, GS, 2, r, W), BF),
            V((M, r, W), BF), V((M - 1, r, W), BF), V((r, W), F32),
            DMA((M - 1,)), DMA((M - 1,)), DMA((M - 1,)), DMA((M - 1,)),
            DMA((PB,)), DMA((PB,)), DMA((PB, GS)), DMA((PB, GS)),
            DMA((M - 1,)), DMA((M - 1,)),
        ],
        compiler_params=pltpu.CompilerParams(
            collective_id=0, has_side_effects=True, vmem_limit_bytes=60 * 1024 * 1024
        ),
    )(latent[0], w_in, w_out, target, cell_mask.reshape(1, N))


def solution(mesh):
    in_specs = (P("member", "cell", None), P(), P(), P(None, "cell"), P("cell"))
    out_specs = (P(("member", "cell"), None), P(("member", "cell"), None))
    return jax.shard_map(
        per_device, mesh=mesh, in_specs=in_specs, out_specs=out_specs, check_vma=False
    )
```

time: 218 us -> 59.9 us (0.27)
  waiting for transfers between devices: 161 us -> 0 us
  Pallas kernels: 0 us -> 53 us
  matrix products: 20.8 us -> 0 us
  between operations: 14.1 us -> 0.64 us
  other arithmetic: 9.23 us -> 0 us
  local copies, waits for them, and re-layouts: 12.5 us -> 5.94 us
    unnamed x3 -> x0, waiting for transfers between devices: 106 us -> none
    all_gather x1 -> x0, waiting for transfers between devices: 54.6 us -> none  [per_device(): lax.all_gather(fields[None], 'member', axis=0, tiled=True)]
    pallas_call x0 -> x1, Pallas kernels: none -> 53 us  [per_device(): pl.pallas_call(functools.partial(body, M, CN), out_shape=(jax.ShapeDtypeS...]
    dot_general x4 -> x0, matrix products: 20.8 us -> none  [the longest x1 10.6 us: per_device(): lax.dot_general(own_latent, grad_pre, (((0,), (0,)), ((), ())), preferred...]
    concatenate x1 -> x0, other arithmetic: 4.99 us -> none  [per_device(): jnp.concatenate([grad_in, grad_out], axis=1)]
    unnamed x15 -> x3, local copies, waits for them, and re-layouts: 9.56 us -> 4.65 us
    reduce_sum x1 -> x0, other arithmetic: 3.06 us -> none  [per_device(): jnp.sum(kernel_fn(wide[None] - lax.all_gather(fields[None], 'member', axi...]
    slice x2 -> x0, local copies, waits for them, and re-layouts: 2.89 us -> none  [per_device(): return (owned[:, :width], owned[:, width:])]
  transfers between devices with their start and end apart: 2 -> 0, of which waited for: 2 -> 0; matrix products, arithmetic and copies ran while one was open for 0% -> 0% of each run, Pallas kernels for 0% -> 0%
where the time goes in v1:
time: 59.9 us; the launch traced here: 59.6 us
  Pallas kernels  53 us (88%)
  local copies, waits for them, and re-layouts  5.94 us (10%)
  between operations  0.64 us (1%)
    pallas_call x1, Pallas kernels, per_device(): pl.pallas_call(functools.partial(body, M, CN), out_shape=(jax.ShapeDtypeS...  53 us
    unnamed x3, local copies, waits for them, and re-layouts  4.65 us
    reshape x1, local copies, waits for them, and re-layouts, per_device(): cell_mask.reshape(1, N)  1.3 us

profile of v1, /device:TPU:0, one launch (start us, length us, event | category | flops | bytes accessed | tf_op | source)
XLA Modules:
  0.0 59.6 jit_solution(9630237181448444780)
XLA Ops:
  0.6 1.3 %reshape.7.mask = s32[1,1536]{1,0:T(1,128)} reshape(s32[1536]{0:T(1024)} %param.9) | data formatting | bytes 12288 | tf_op jit(solution)/shard_map/reshape | solution.py:290
  1.9 1.8 %copy.7.w_out = bf16[1024,96]{1,0:T(8,128)(2,1)} copy(bf16[1024,96]{0,1:T(8,128)(2,1)} %param.7) | data formatting | bytes 393216 | tf_op args[2]
  3.7 53.0 %shard_map.68 = (f32[32,1024]{1,0:T(8,128)}, f32[32,96]{1,0:T(8,128)}) custom-call(bf16[1536,1024]{1,0:T(8,128)(2,1)} %bitcast.1, bf16[1024,1024]{1,0:T(8,128)(2,1)} %w_in.1, bf16[1024,96]{1,0:T(8,128)(2,1)} %copy.7.w_out, bf16[96,1536]{1,0:T(8,128)(2,1)} %target.1, s32[1,1536]{1,0:T(1,128)} %reshape.7.mask), custom_call_target="tpu_custom_call" | custom-call | tf_op jit(solution)/shard_map/pallas_call | solution.py:268
  56.7 1.6 %copy.10 = f32[32,1024]{1,0:T(8,128)} copy(f32[32,1024]{1,0:T(8,128)} %get-tuple-element.4) | data formatting | bytes 262144
  58.3 1.3 %copy.11 = f32[32,96]{1,0:T(8,128)} copy(f32[32,96]{1,0:T(8,128)} %get-tuple-element.5) | data formatting | bytes 24576

commit v2 on v1

--- a/solution.py
+++ b/solution.py
@@ -26,11 +26,11 @@
 
 def body(
     M, CN,
-    lat, w_in, w_out, target, mask, out_in, out_out,
-    pre, hid, gp, lat_t, hid_t, tgt_t, wgt_t,
+    lat_hbm, w_in_hbm, w_out, target, mask, out_in, out_out,
+    lat, w_in, slope, hid, gp, sums, tgt_t, wgt_t,
     fsend, frecv, gsend, gf,
     acc_f, acc_b, r1, k2, s2, r2, s3, r3, k3,
-    sem_fs, sem_fr, sem_gs, sem_gr, sem1s, sem1r, sem2s, sem2r, sem3s, sem3r,
+    sem_in, sem_fs, sem_fr, sem_gs, sem_gr, sem1s, sem1r, sem2s, sem2r, sem3s, sem3r,
 ):
     me = lax.axis_index("member")
     cell = lax.axis_index("cell")
@@ -39,11 +39,23 @@
     G = CN // 2
     N, D = lat.shape
     H = w_in.shape[1]
-    FD = w_out.shape[1]
+    FD = w_out.shape[0]
     C = N // M
     PB = M // 2
     r = D // (M * CN)
     scale = 1.0 / (float(N * CN) ** 0.5) / M
+
+    def block_of(i):
+        return lax.rem(me // 2 + 1 + i, PB)
+
+    def load(i):
+        rows = pl.ds(pl.multiple_of(block_of(i) * (2 * C), 2 * C), 2 * C)
+        return pltpu.make_async_copy(lat_hbm.at[rows, :], lat.at[rows, :], sem_in.at[i])
+
+    load_w = pltpu.make_async_copy(w_in_hbm, w_in, sem_in.at[PB])
+    load_w.start()
+    for i in range(PB):
+        load(i).start()
 
     barrier = pltpu.get_barrier_semaphore()
     for d in range(1, M):
@@ -53,6 +65,13 @@
         pl.semaphore_signal(
             barrier, inc=1, device_id=(me, lax.rem(grp + d, G) * 2 + core), device_id_type=MESH
         )
+
+    for b in range(N // 128):
+        cols = slice(128 * b, 128 * b + 128)
+        tgt_t[cols, :] = target[:, cols].astype(F32).T
+        w = mask[cols].astype(F32) * scale
+        wgt_t[cols, :] = jnp.broadcast_to(w[None, :], (8, 128)).T
+
     pl.semaphore_wait(barrier, M - 1 + 1 + G - 1)
 
     def peer(d):
@@ -89,18 +108,19 @@
             s3.at[t], r3.at[d - 1], sem3s.at[d - 1], sem3r.at[d - 1],
             device_id=(t, cell), device_id_type=MESH,
         )
-
-    def block_of(i):
-        return lax.rem(me // 2 + 1 + i, PB)
 
     def forward(i, carry):
         p = block_of(i)
         rows = pl.ds(pl.multiple_of(p * (2 * C), 2 * C), 2 * C)
+        load(i).wait()
         v = mm(lat[rows, :], w_in[...])
-        pre[rows, :] = v
-        h = (v * sigmoid(v)).astype(BF)
+        s = sigmoid(v)
+        slope[rows, :] = s * (1.0 + v * (1.0 - s))
+        h = (v * s).astype(BF)
         hid[rows, :] = h
-        f = mm(h, w_out[...]).astype(BF)
+        f = lax.dot_general(
+            h, w_out[...], (((1,), (1,)), ((), ())), preferred_element_type=F32
+        ).astype(BF)
         fsend[2 * p] = f[:C]
         fsend[2 * p + 1] = f[C:]
         for s in range(2):
@@ -112,18 +132,10 @@
 
         return carry
 
+    load_w.wait()
     lax.fori_loop(0, PB, forward, 0)
 
-    wrow = mask[...].astype(F32) * scale
-    for b in range(N // 128):
-        cols = slice(128 * b, 128 * b + 128)
-        tgt_t[cols, :] = target[:, cols].astype(F32).T
-        wgt_t[cols, :] = jnp.broadcast_to(wrow[:, cols], (8, 128)).T
-
-    for b in range(N // 128):
-        cols = slice(128 * b, 128 * b + 128)
-        lat_t[:, cols] = lat[cols, :].T
-
+    sums[...] = jnp.zeros_like(sums)
     for d in range(1, M):
         f_copy(d).wait_recv()
 
@@ -152,39 +164,61 @@
 
     lax.fori_loop(0, C // RB, pairs, 0)
 
-    for d in range(1, M):
-        g_copy(d).start()
-
-    for b in range(N // 128):
-        cols = slice(128 * b, 128 * b + 128)
-        hid_t[:, cols] = hid[cols, :].T
-
-    def back(j):
-        rows = pl.ds(pl.multiple_of(j * C, C), C)
-        q = lax.dot_general(gf[j], w_out[...], (((1,), (1,)), ((), ())), preferred_element_type=F32)
-        v = pre[rows, :]
-        s = sigmoid(v)
-        gp[rows, :] = (q * (s * (1.0 + v * (1.0 - s)))).astype(BF)
-
-    back(me)
-
-    def backs(d, carry):
-        pltpu.make_async_remote_copy(
-            gsend.at[d - 1], gf.at[lax.rem(me + d, M)], sem_gs.at[d - 1], sem_gr.at[d - 1],
-            device_id=(peer(d), cell), device_id_type=MESH,
-        ).wait_recv()
-        back(lax.rem(me + d, M))
+    g_copy(lax.rem(me - (me + 1 - 2 * lax.rem(me, 2)) + M, M)).start()
+    for i in range(1, PB):
+        p = lax.rem(me // 2 - i + PB, PB)
+        for e in range(2):
+            g_copy(lax.rem(me - (2 * p + e) + M, M)).start()
+
+    T = 2 * r * CN
+
+    def tile(p, q):
+        rows = pl.ds(pl.multiple_of(p * (2 * C), 2 * C), 2 * C)
+        cols = pl.ds(pl.multiple_of(q * T, T), T)
+        over = (((0,), (0,)), ((), ()))
+        g = gf[pl.ds(2 * p, 2)].reshape(2 * C, FD)
+        a = lax.dot_general(lat[rows, cols], gp[rows, :], over, preferred_element_type=F32)
+        b = lax.dot_general(hid[rows, cols], g, over, preferred_element_type=F32)
+        to = pl.ds(pl.multiple_of(q * T, T), T)
+        return a + sums[to, :H], b + sums[to, H : H + FD]
+
+    def backs(k, carry):
+        p = lax.rem(me // 2 + k, PB)
+        for e in range(2):
+            j = 2 * p + e
+
+            @pl.when(j != me)
+            def _():
+                d = lax.rem(j - me + M, M)
+                pltpu.make_async_remote_copy(
+                    gsend.at[d - 1], gf.at[j], sem_gs.at[d - 1], sem_gr.at[d - 1],
+                    device_id=(j, cell), device_id_type=MESH,
+                ).wait_recv()
+
+        rows = pl.ds(pl.multiple_of(p * (2 * C), 2 * C), 2 * C)
+        g = gf[pl.ds(2 * p, 2)].reshape(2 * C, FD)
+        gp[rows, :] = (mm(g, w_out[...]) * slope[rows, :]).astype(BF)
+
+        @pl.when(k < PB - 1)
+        def _():
+            def more(q, c):
+                a, b = tile(p, q)
+                to = pl.ds(pl.multiple_of(q * T, T), T)
+                sums[to, :H] = a
+                sums[to, H : H + FD] = b
+                return c
+
+            lax.fori_loop(0, PB, more, 0)
+
         return carry
 
-    lax.fori_loop(1, M, backs, 0)
+    lax.fori_loop(0, PB, backs, 0)
 
     def step(i, carry):
         @pl.when(i < PB)
         def _():
             p = block_of(i)
-            rows = pl.ds(pl.multiple_of(p * (2 * r * CN), 2 * r * CN), 2 * r * CN)
-            a = mm(lat_t[rows, :], gp[...])
-            b = mm(hid_t[rows, :], gf[...].reshape(N, FD))
+            a, b = tile(lax.rem(me // 2 + PB - 1, PB), p)
             for s in range(2):
                 for c in range(CN):
                     at = (s * CN + c) * r
@@ -271,23 +305,23 @@
             jax.ShapeDtypeStruct((r, H), F32),
             jax.ShapeDtypeStruct((r, FD), F32),
         ),
-        in_specs=[vm] * 5,
+        in_specs=[pl.BlockSpec(memory_space=pl.ANY)] * 2 + [vm] * 3,
         out_specs=(vm, vm),
         scratch_shapes=[
-            V((N, H), F32), V((N, H), BF), V((N, H), BF), V((D, N), BF), V((H, N), BF),
+            V((N, D), BF), V((D, H), BF), V((N, H), F32), V((N, H), BF), V((N, H), BF), V((D, W), F32),
             V((N, FD), F32), V((N, 8), F32),
             V((M, C, FD), BF), V((M - 1, C, FD), BF), V((M - 1, C, FD), BF), V((M, C, FD), BF),
             V((PB, 2, 2, G, r, W), F32), V((PB, 2, 2, G, r, W), BF), V((PB, 2, G, r, W), BF),
             V((PB, G, 2, r, W), F32), V((PB, G, 2, r, W), BF), V((PB, GS, 2, r, W), BF),
             V((M, r, W), BF), V((M - 1, r, W), BF), V((r, W), F32),
-            DMA((M - 1,)), DMA((M - 1,)), DMA((M - 1,)), DMA((M - 1,)),
+            DMA((PB + 1,)), DMA((M - 1,)), DMA((M - 1,)), DMA((M - 1,)), DMA((M - 1,)),
             DMA((PB,)), DMA((PB,)), DMA((PB, GS)), DMA((PB, GS)),
             DMA((M - 1,)), DMA((M - 1,)),
         ],
         compiler_params=pltpu.CompilerParams(
             collective_id=0, has_side_effects=True, vmem_limit_bytes=60 * 1024 * 1024
         ),
-    )(latent[0], w_in, w_out, target, cell_mask.reshape(1, N))
+    )(latent[0], w_in, w_out.T, target, cell_mask)
 
 
 def solution(mesh):

time: 59.9 us -> 57.6 us (0.962)
  local copies, waits for them, and re-layouts: 5.94 us -> 2.89 us
  Pallas kernels: 53 us -> 53.9 us
    unnamed x3 -> x2, local copies, waits for them, and re-layouts: 4.65 us -> 2.89 us
    reshape x1 -> x0, local copies, waits for them, and re-layouts: 1.3 us -> none  [per_device(): cell_mask.reshape(1, N)]
    pallas_call x1, Pallas kernels: 53 us -> 53.9 us  [per_device(): pl.pallas_call(functools.partial(body, M, CN), out_shape=(jax.ShapeDtypeS...]
where the time goes in v2:
time: 57.6 us; the launch traced here: 57.4 us
  Pallas kernels  53.9 us (94%)
  local copies, waits for them, and re-layouts  2.89 us (5%)
  between operations  0.64 us (1%)
    pallas_call x1, Pallas kernels, per_device(): pl.pallas_call(functools.partial(body, M, CN), out_shape=(jax.ShapeDtypeS...  53.9 us
    unnamed x2, local copies, waits for them, and re-layouts  2.89 us

profile of v2, /device:TPU:0, one launch (start us, length us, event | category | flops | bytes accessed | tf_op | source)
XLA Modules:
  0.0 57.4 jit_solution(343360717787233429)
XLA Ops:
  0.6 53.9 %shard_map.68 = (f32[32,1024]{1,0:T(8,128)}, f32[32,96]{1,0:T(8,128)}) custom-call(bf16[1536,1024]{1,0:T(8,128)(2,1)} %bitcast.2, bf16[1024,1024]{1,0:T(8,128)(2,1)} %w_in_hbm.1, bf16[96,1024]{1,0:T(8,128)(2,1)} %bitcast.3, bf16[96,1536]{1,0:T(8,128)(2,1)} %target.1, s32[1536]{0:T(1024)} %mask.1), custom_call_target="tpu_custom_call" | custom-call | tf_op jit(solution)/shard_map/pallas_call | solution.py:302
  54.5 1.6 %copy.9 = f32[32,1024]{1,0:T(8,128)} copy(f32[32,1024]{1,0:T(8,128)} %get-tuple-element.4) | data formatting | bytes 262144
  56.1 1.3 %copy.10 = f32[32,96]{1,0:T(8,128)} copy(f32[32,96]{1,0:T(8,128)} %get-tuple-element.5) | data formatting | bytes 24576

commit v3 on v1

--- a/solution.py
+++ b/solution.py
@@ -26,11 +26,11 @@
 
 def body(
     M, CN,
-    lat, w_in, w_out, target, mask, out_in, out_out,
-    pre, hid, gp, lat_t, hid_t, tgt_t, wgt_t,
+    lat_hbm, w_in_hbm, w_out, target, mask, out_in, out_out,
+    lat, w_in, slope, hid, gp, lat_t, hid_t, tgt_t, wgt_t,
     fsend, frecv, gsend, gf,
     acc_f, acc_b, r1, k2, s2, r2, s3, r3, k3,
-    sem_fs, sem_fr, sem_gs, sem_gr, sem1s, sem1r, sem2s, sem2r, sem3s, sem3r,
+    sem_in, sem_fs, sem_fr, sem_gs, sem_gr, sem1s, sem1r, sem2s, sem2r, sem3s, sem3r,
 ):
     me = lax.axis_index("member")
     cell = lax.axis_index("cell")
@@ -39,11 +39,23 @@
     G = CN // 2
     N, D = lat.shape
     H = w_in.shape[1]
-    FD = w_out.shape[1]
+    FD = w_out.shape[0]
     C = N // M
     PB = M // 2
     r = D // (M * CN)
     scale = 1.0 / (float(N * CN) ** 0.5) / M
+
+    def block_of(i):
+        return lax.rem(me // 2 + 1 + i, PB)
+
+    def load(i):
+        rows = pl.ds(pl.multiple_of(block_of(i) * (2 * C), 2 * C), 2 * C)
+        return pltpu.make_async_copy(lat_hbm.at[rows, :], lat.at[rows, :], sem_in.at[i])
+
+    load_w = pltpu.make_async_copy(w_in_hbm, w_in, sem_in.at[PB])
+    load_w.start()
+    for i in range(PB):
+        load(i).start()
 
     barrier = pltpu.get_barrier_semaphore()
     for d in range(1, M):
@@ -53,6 +65,13 @@
         pl.semaphore_signal(
             barrier, inc=1, device_id=(me, lax.rem(grp + d, G) * 2 + core), device_id_type=MESH
         )
+
+    for b in range(N // 128):
+        cols = slice(128 * b, 128 * b + 128)
+        tgt_t[cols, :] = target[:, cols].astype(F32).T
+        w = mask[cols].astype(F32) * scale
+        wgt_t[cols, :] = jnp.broadcast_to(w[None, :], (8, 128)).T
+
     pl.semaphore_wait(barrier, M - 1 + 1 + G - 1)
 
     def peer(d):
@@ -89,18 +108,19 @@
             s3.at[t], r3.at[d - 1], sem3s.at[d - 1], sem3r.at[d - 1],
             device_id=(t, cell), device_id_type=MESH,
         )
-
-    def block_of(i):
-        return lax.rem(me // 2 + 1 + i, PB)
 
     def forward(i, carry):
         p = block_of(i)
         rows = pl.ds(pl.multiple_of(p * (2 * C), 2 * C), 2 * C)
+        load(i).wait()
         v = mm(lat[rows, :], w_in[...])
-        pre[rows, :] = v
-        h = (v * sigmoid(v)).astype(BF)
+        s = sigmoid(v)
+        slope[rows, :] = s * (1.0 + v * (1.0 - s))
+        h = (v * s).astype(BF)
         hid[rows, :] = h
-        f = mm(h, w_out[...]).astype(BF)
+        f = lax.dot_general(
+            h, w_out[...], (((1,), (1,)), ((), ())), preferred_element_type=F32
+        ).astype(BF)
         fsend[2 * p] = f[:C]
         fsend[2 * p + 1] = f[C:]
         for s in range(2):
@@ -112,13 +132,8 @@
 
         return carry
 
+    load_w.wait()
     lax.fori_loop(0, PB, forward, 0)
-
-    wrow = mask[...].astype(F32) * scale
-    for b in range(N // 128):
-        cols = slice(128 * b, 128 * b + 128)
-        tgt_t[cols, :] = target[:, cols].astype(F32).T
-        wgt_t[cols, :] = jnp.broadcast_to(wrow[:, cols], (8, 128)).T
 
     for b in range(N // 128):
         cols = slice(128 * b, 128 * b + 128)
@@ -161,10 +176,7 @@
 
     def back(j):
         rows = pl.ds(pl.multiple_of(j * C, C), C)
-        q = lax.dot_general(gf[j], w_out[...], (((1,), (1,)), ((), ())), preferred_element_type=F32)
-        v = pre[rows, :]
-        s = sigmoid(v)
-        gp[rows, :] = (q * (s * (1.0 + v * (1.0 - s)))).astype(BF)
+        gp[rows, :] = (mm(gf[j], w_out[...]) * slope[rows, :]).astype(BF)
 
     back(me)
 
@@ -271,23 +283,23 @@
             jax.ShapeDtypeStruct((r, H), F32),
             jax.ShapeDtypeStruct((r, FD), F32),
         ),
-        in_specs=[vm] * 5,
+        in_specs=[pl.BlockSpec(memory_space=pl.ANY)] * 2 + [vm] * 3,
         out_specs=(vm, vm),
         scratch_shapes=[
-            V((N, H), F32), V((N, H), BF), V((N, H), BF), V((D, N), BF), V((H, N), BF),
+            V((N, D), BF), V((D, H), BF), V((N, H), F32), V((N, H), BF), V((N, H), BF), V((D, N), BF), V((H, N), BF),
             V((N, FD), F32), V((N, 8), F32),
             V((M, C, FD), BF), V((M - 1, C, FD), BF), V((M - 1, C, FD), BF), V((M, C, FD), BF),
             V((PB, 2, 2, G, r, W), F32), V((PB, 2, 2, G, r, W), BF), V((PB, 2, G, r, W), BF),
             V((PB, G, 2, r, W), F32), V((PB, G, 2, r, W), BF), V((PB, GS, 2, r, W), BF),
             V((M, r, W), BF), V((M - 1, r, W), BF), V((r, W), F32),
-            DMA((M - 1,)), DMA((M - 1,)), DMA((M - 1,)), DMA((M - 1,)),
+            DMA((PB + 1,)), DMA((M - 1,)), DMA((M - 1,)), DMA((M - 1,)), DMA((M - 1,)),
             DMA((PB,)), DMA((PB,)), DMA((PB, GS)), DMA((PB, GS)),
             DMA((M - 1,)), DMA((M - 1,)),
         ],
         compiler_params=pltpu.CompilerParams(
             collective_id=0, has_side_effects=True, vmem_limit_bytes=60 * 1024 * 1024
         ),
-    )(latent[0], w_in, w_out, target, cell_mask.reshape(1, N))
+    )(latent[0], w_in, w_out.T, target, cell_mask)
 
 
 def solution(mesh):

time: 59.9 us -> 55.5 us (0.927)
  local copies, waits for them, and re-layouts: 5.94 us -> 2.89 us
  Pallas kernels: 53 us -> 51.7 us
    unnamed x3 -> x2, local copies, waits for them, and re-layouts: 4.65 us -> 2.89 us
    pallas_call x1, Pallas kernels: 53 us -> 51.7 us  [per_device(): pl.pallas_call(functools.partial(body, M, CN), out_shape=(jax.ShapeDtypeS...]
    reshape x1 -> x0, local copies, waits for them, and re-layouts: 1.3 us -> none  [per_device(): cell_mask.reshape(1, N)]
where the time goes in v3:
time: 55.5 us; the launch traced here: 55.2 us
  Pallas kernels  51.7 us (93%)
  local copies, waits for them, and re-layouts  2.89 us (5%)
  between operations  0.64 us (1%)
    pallas_call x1, Pallas kernels, per_device(): pl.pallas_call(functools.partial(body, M, CN), out_shape=(jax.ShapeDtypeS...  51.7 us
    unnamed x2, local copies, waits for them, and re-layouts  2.89 us

profile of v3, /device:TPU:0, one launch (start us, length us, event | category | flops | bytes accessed | tf_op | source)
XLA Modules:
  0.0 55.2 jit_solution(1186528827216810116)
XLA Ops:
  0.6 51.7 %shard_map.68 = (f32[32,1024]{1,0:T(8,128)}, f32[32,96]{1,0:T(8,128)}) custom-call(bf16[1536,1024]{1,0:T(8,128)(2,1)} %bitcast.2, bf16[1024,1024]{1,0:T(8,128)(2,1)} %w_in_hbm.1, bf16[96,1024]{1,0:T(8,128)(2,1)} %bitcast.3, bf16[96,1536]{1,0:T(8,128)(2,1)} %target.1, s32[1536]{0:T(1024)} %mask.1), custom_call_target="tpu_custom_call" | custom-call | tf_op jit(solution)/shard_map/pallas_call | solution.py:280
  52.3 1.6 %copy.9 = f32[32,1024]{1,0:T(8,128)} copy(f32[32,1024]{1,0:T(8,128)} %get-tuple-element.4) | data formatting | bytes 262144
  53.9 1.3 %copy.10 = f32[32,96]{1,0:T(8,128)} copy(f32[32,96]{1,0:T(8,128)} %get-tuple-element.5) | data formatting | bytes 24576
